TPU v7x, 256 devices: a whole 4x4x8 slice. The times are simulated.
256 devices in a mesh: frame: 32 (over y, z), coord: 8 (over x, core).
Axes of the slice: x: 4, y: 4, z: 8, core: 2. Of those that a mesh axis runs over, the one named last changes fastest.
Arguments:
- frames: bfloat16 [32768, 4224], P('frame'), may hold values from -0.5 to 1.5
- b_values: bfloat16 [4096, 512], P('coord'), may hold values from -0.25 to 0.25
- b_cols: int32 [64, 8], P('coord'), may hold values from 0 to 65, as said below
- frame_window: int32 [32768], P('frame'), may hold values from 0 to 1, as said below
Outputs:
- count: float32 [], replicated
- mean: float32 [4096], P('coord')
- covariance: float32 [4096, 4096], P('frame', 'coord')
Inputs may be any that keep to these rules, and one draw needn't show every extreme that they name: `b_cols`: each row holds 8 different column-block indices. `frame_window`: the first and the last frame are always in the window.
All inputs are finite; a program needn't handle non-finite values.
Results may differ from a plain program's by a relative error of at most 0.0022.
Values may be sent and summed in bfloat16 or wider, within the bound.
A program may use at most 128 MiB of HBM per device.

v0:
```python
import jax
import jax.numpy as jnp
from jax import lax
from jax.sharding import PartitionSpec as P

BLOCK = 64


def project(frames, values, col_blocks):
    frame_rows = frames.shape[0]
    blocks = frames.reshape(frame_rows, -1, BLOCK)
    picked = jnp.take(blocks, col_blocks, axis=1)
    panel = values.reshape(col_blocks.shape[0], BLOCK, col_blocks.shape[1], BLOCK)
    product = jnp.einsum("frkc,rjkc->frj", picked, panel, preferred_element_type=jnp.float32)
    return product.reshape(frame_rows, -1).astype(jnp.bfloat16)


def on_device(frames, b_values, b_cols, frame_window):
    weight = frame_window.astype(jnp.float32)
    weight_half = frame_window.astype(jnp.bfloat16)
    coords_mine = project(frames, b_values, b_cols)
    local_count = jnp.sum(weight)
    local_sums = jnp.dot(weight_half, coords_mine, preferred_element_type=jnp.float32)
    count, col_sums = lax.psum((local_count, local_sums), "frame")
    mean_mine = col_sums / count
    centered_mine = (weight[:, None] * (coords_mine.astype(jnp.float32) - mean_mine)).astype(
        jnp.bfloat16
    )
    centered_full = lax.all_gather(centered_mine, "coord", axis=1, tiled=True)
    gram_share = lax.psum_scatter(
        lax.dot_general(
            centered_full,
            centered_mine,
            (((0,), (0,)), ((), ())),
            preferred_element_type=jnp.float32,
        ),
        "frame",
        scatter_dimension=0,
        tiled=True,
    )
    covariance = gram_share / (count - 1.0)
    return (count, mean_mine, covariance)


def solution(mesh):
    return jax.shard_map(
        on_device,
        mesh=mesh,
        in_specs=(P("frame", None), P("coord", None), P("coord", None), P("frame")),
        out_specs=(P(), P("coord"), P("frame", "coord")),
        check_vma=False,
    )
```

profile of v0, /device:TPU:6, one launch (start us, length us, event | category | flops | bytes accessed | tf_op | source)
XLA Modules:
  0.0 414.5 jit_solution(17868845092347581777)
XLA Ops:
  7.2 0.0 all-gather.2.cloned.1.call-start
  7.2 0.7 compare_select_fusion
  7.9 0.7 compare_and_fusion
  8.6 0.8 fusion.9
  9.4 1.3 convert_reduce_fusion
  10.7 12.4 %copy.9 = bf16[1024,4224]{0,1:T(8,128)(2,1)} copy(bf16[1024,4224]{1,0:T(8,128)(2,1)} %param.4) | data formatting | bytes 17301504 | tf_op args[0]
  23.0 0.1 reshape.25
  23.1 0.0 copy-done
  23.1 0.5 reshape.22
  23.7 9.0 %gather_fusion = bf16[64,1024,64]{1,2,0:T(8,128)(2,1)} fusion(bf16[1024,66,64]{0,2,1:T(8,128)(2,1)} %bitcast.19, s32[1024]{0:T(1024)S(1)} %pad_clamp_fusion), kind=kCustom, calls=%fused_computation | custom fusion | bytes 16777472 | tf_op jit(solution)/shard_map/jit(_take)/gather | solution.py:12
  32.7 5.4 %bitcast_convert_fusion = bf16[8,1024,64]{1,2,0:T(8,128)(2,1)S(1)} fusion(bf16[8,8,1024,64]{2,3,1,0:T(8,128)(2,1)} %bitcast.20, pred[8,8]{1,0:T(8,128)(4,1)S(1)} %compare_and_fusion, bf16[8,64,8,64]{3,2,1,0:T(8,128)(2,1)S(1)} %reshape.22), kind=kOutput, calls=%fused_computation.6 | convolution fusion | flops 541589504 | bytes 9961536 | tf_op jit(solution)/shard_map/frkc,rjkc->frj/dot_general | solution.py:14
  38.1 0.4 fusion.10
  38.5 78.6 %all-reduce = (f32[]{:T(128)}, f32[512]{0:T(512)S(1)}) all-reduce(f32[]{:T(128)} %convert_reduce_fusion, f32[512]{0:T(512)S(1)} %bitcast.22), channel_id=1, replica_groups=mesh['frame'=32,'coord'=8] {'frame'}, use_global_device_ids=true, to_apply=%region_1.2 | all-reduce | flops 513 | bytes 4104 | tf_op jit(solution)/shard_map/psum | solution.py:24
  117.1 0.6 broadcast_divide_fusion.1
  117.7 0.0 copy-start.1
  117.7 1.3 multiply_convert_fusion
  119.0 0.0 all-gather.2.cloned.1.call-update
  119.1 0.0 reduce-scatter.2.cloned.1.call-start
  119.1 44.2 %all-gather.2.cloned.1.call-done = bf16[1024,4096]{0,1:T(8,128)(2,1)} async-done(((bf16[1024,512]{0,1:T(8,128)(2,1)}), bf16[1024,4096]{0,1:T(8,128)(2,1)}) %all-gather.2.cloned.1.call-update) | async-done | bytes 8388624 | tf_op jit(solution)/shard_map/all_gather | solution.py:29
  163.3 11.4 %fusion.11 = f32[4096,512]{1,0:T(8,128)} fusion(bf16[1024,4096]{0,1:T(8,128)(2,1)} %all-gather.2.cloned.1.call-done, bf16[1024,512]{0,1:T(8,128)(2,1)} %multiply_convert_fusion), kind=kOutput, calls=%fused_computation.18 | convolution fusion | flops 4294967296 | bytes 17825792 | tf_op jit(solution)/shard_map/dot_general | solution.py:31
  174.7 0.0 copy-done.1
  174.7 0.0 reduce-scatter.2.cloned.1.call-update
  175.3 230.6 %reduce-scatter.2.cloned.1.call-done = f32[128,512]{1,0:T(8,128)} async-done(((f32[4096,512]{1,0:T(8,128)}), f32[128,512]{1,0:T(8,128)}) %reduce-scatter.2.cloned.1.call-update) | async-done | bytes 262160 | tf_op jit(solution)/shard_map/reduce_scatter | solution.py:30
  406.0 1.7 broadcast_divide_fusion
  (3 shorter events, 0.0 us)
Async XLA Ops:
  7.2 156.1 %all-gather.2.cloned.1.call-start = ((), (), s32[]{:S(2)}) async-start(), calls=%async_computation.1 | async-start | bytes 9437184 | tf_op jit(solution)/shard_map/all_gather | solution.py:29
  10.7 12.5 %copy-start = (bf16[512,512]{1,0:T(8,128)(2,1)S(1)}, bf16[512,512]{1,0:T(8,128)(2,1)}, u32[]{:S(2)}) copy-start(bf16[512,512]{1,0:T(8,128)(2,1)} %param.5) | copy-start | bytes 1572868
  117.7 56.9 %copy-start.1 = (f32[512]{0:T(512)}, f32[512]{0:T(512)S(1)}, u32[]{:S(2)}) copy-start(f32[512]{0:T(512)S(1)} %broadcast_divide_fusion.1) | copy-start | bytes 6148
  119.1 286.9 %reduce-scatter.2.cloned.1.call-start = ((), (), s32[]{:S(2)}) async-start(), calls=%async_computation.2 | async-start | bytes 8650752 | tf_op jit(solution)/shard_map/reduce_scatter | solution.py:30
Sparse Core Ops, SparseCore 0:
  119.2 44.0 all-gather.1
  174.8 231.1 reduce-scatter.1
where the time goes:
time: 415 us; the launch traced here: 414 us
  waiting for transfers between devices  275 us (66%)
  blocking collectives  78.6 us (19%)
  local copies, waits for them, and re-layouts  22 us (5%)
  matrix products  17.2 us (4%)
  between operations  14.7 us (4%)
  other arithmetic  7.07 us (2%)
    reduce_scatter x1, waiting for transfers between devices, on_device(): lax.psum_scatter(lax.dot_general(centered_full, centered_mine, (((0,), (0...  231 us
    psum x1, blocking collectives, on_device(): count, col_sums = lax.psum((local_count, local_sums), 'frame')  78.6 us
    all_gather x1, waiting for transfers between devices, on_device(): centered_full = lax.all_gather(centered_mine, 'coord', axis=1, tiled=True)  44.2 us
    unnamed x5, local copies, waits for them, and re-layouts  12.4 us
    dot_general x1, matrix products, on_device(): lax.dot_general(centered_full, centered_mine, (((0,), (0,)), ((), ())), p...  11.4 us
    gather x1, local copies, waits for them, and re-layouts, project(): picked = jnp.take(blocks, col_blocks, axis=1)  9.02 us
  transfers between devices with their start and end apart: 2, of which 2 were waited for; matrix products, arithmetic and copies ran while one was open for 0% of the time, Pallas kernels for 0%

commit v1 on v0

v1 whole, which is shorter than its diff:
```python
import functools

import jax
import jax.numpy as jnp
from jax import lax
from jax.experimental import pallas as pl
from jax.experimental.pallas import tpu as pltpu
from jax.sharding import PartitionSpec as P

BLOCK = 64
NY, NZ, NX = 4, 8, 4
NF, NC = NY * NZ, NX * 2
PANEL = 512
OWN = 128
MESH = pl.DeviceIdType.MESH
BF = jnp.bfloat16
F32 = jnp.float32


def densify(cols_ref, vals_ref, out_ref):
    out_ref[...] = jnp.zeros_like(out_ref)
    turned = vals_ref[...].T
    for r in range(8):
        lanes = slice(r * BLOCK, (r + 1) * BLOCK)
        for k in range(8):
            row = pl.multiple_of(cols_ref[r, k] * BLOCK, BLOCK)
            out_ref[pl.ds(row, BLOCK), lanes] = turned[k * BLOCK : (k + 1) * BLOCK, lanes]


def remote(src, dst, send_sem, recv_sem, device):
    return pltpu.make_async_remote_copy(
        src_ref=src, dst_ref=dst, send_sem=send_sem, recv_sem=recv_sem, device_id=device, device_id_type=MESH
    )


class Ring:
    def __init__(self, n, pos, peer, own, recv, send_sems, recv_sems, rows):
        self.n, self.pos, self.own, self.recv = n, pos, own, recv
        self.peer = [peer(lax.rem(pos + 1, n)), peer(lax.rem(pos + n - 1, n))]
        self.send_sems, self.recv_sems, self.rows = send_sems, recv_sems, rows
        self.half = [slice(rows // 2, rows), slice(0, rows // 2)]

    def target(self, d, s):
        steps = self.n // 2 - s
        return lax.rem(self.pos + (steps if d == 0 else self.n - steps), self.n)

    def copy(self, d, s):
        t = self.target(d, s)
        if s == 0:
            src = self.own.at[t, self.half[d]]
            dst = self.recv.at[d, 0, self.half[d]]
        else:
            src = self.recv.at[d, s - 1]
            dst = self.recv.at[d, s]
        return remote(src, dst, self.send_sems.at[d, s], self.recv_sems.at[d, s], self.peer[d])

    def start(self, d, s):
        if s > 0:
            self.copy(d, s - 1).wait_recv()
            t = self.target(d, s)
            buf = self.recv.at[d, s - 1]
            if s == 1:
                h, o = self.half[d], self.half[1 - d]
                buf[h] = (buf[h].astype(F32) + self.own[t, h].astype(F32)).astype(BF)
                buf[o] = self.own[t, o]
            else:
                buf[...] = (buf[...].astype(F32) + self.own[t].astype(F32)).astype(BF)
        self.copy(d, s).start()

    def finish(self):
        last = self.n // 2 - 1
        for d in range(2):
            self.copy(d, last).wait_recv()

    def total(self, sl=slice(None)):
        last = self.n // 2 - 1
        return (
            self.own[self.pos, sl].astype(F32) + self.recv[0, last, sl].astype(F32) + self.recv[1, last, sl].astype(F32)
        )

    def drain(self):
        for d in range(2):
            for s in range(self.n // 2):
                self.copy(d, s).wait_send()


def main_kernel(
    x_hbm, bdt_hbm, vals_ref, cols_ref, wrow_ref,
    count_ref, mean_ref, cov_ref,
    x, bdt, q, g, ball, cbuf, csm, sz, sy, xm, pa, pb, ra, rb, ay, az, bz, by,
    ld_sem, loc_sem, val_s, val_r, col_s, col_r, z_s, z_r, y_s, y_r,
    ay_s, ay_r, az_s, az_r, bz_s, bz_r, by_s, by_r,
):
    f, c = lax.axis_index("frame"), lax.axis_index("coord")
    yy, zz = f // NZ, lax.rem(f, NZ)
    xx, kk = c // 2, lax.rem(c, 2)
    rows_total = x.shape[0]
    XT = 4
    xr = rows_total // XT
    loads = [pltpu.make_async_copy(bdt_hbm, bdt, ld_sem.at[0])]
    for i in range(XT):
        sl = pl.ds(i * xr, xr)
        loads.append(pltpu.make_async_copy(x_hbm.at[sl], x.at[sl], ld_sem.at[i + 1]))
    for cp in loads:
        cp.start()

    def coord_peer(o):
        return (f, lax.rem(c + o, NC))

    def z_peer(o):
        return (yy * NZ + lax.rem(zz + o, NZ), c)

    def y_peer(o):
        return (lax.rem(yy + o, NY) * NZ + zz, c)

    x_up = (f, lax.rem(xx + 1, NX) * 2 + kk)
    x_dn = (f, lax.rem(xx + NX - 1, NX) * 2 + kk)
    sib = (f, xx * 2 + 1 - kk)

    barrier = pltpu.get_barrier_semaphore()
    peers = [coord_peer(o) for o in range(1, NC)] + [z_peer(o) for o in range(1, NZ)] + [y_peer(o) for o in range(1, NY)]
    for p in peers:
        pl.semaphore_signal(barrier, inc=1, device_id=p, device_id_type=MESH)
    pl.semaphore_wait(barrier, len(peers))

    c_up, c_dn, c_op = x_up[1], x_dn[1], lax.rem(c + 4, NC)
    lo, hi = pl.ds(0, 4), pl.ds(4, 4)
    own_vals = pltpu.make_async_copy(vals_ref, ball.at[c], loc_sem.at[0])
    own_cols = pltpu.make_async_copy(cols_ref, cbuf.at[c], loc_sem.at[1])
    own_vals.start()
    own_cols.start()
    v_up = remote(vals_ref, ball.at[c], val_s.at[0], val_r.at[0], x_up)
    v_dn = remote(vals_ref, ball.at[c], val_s.at[1], val_r.at[1], x_dn)
    v_sib = remote(vals_ref, ball.at[c], val_s.at[2], val_r.at[2], sib)
    for cp in (v_up, v_dn, v_sib):
        cp.start()
    col_copies = [
        remote(cols_ref, cbuf.at[c], col_s.at[o - 1], col_r.at[o - 1], coord_peer(o)) for o in range(1, NC)
    ]
    for cp in col_copies:
        cp.start()

    loads[0].wait()
    wrow = wrow_ref[...].astype(F32)
    sums = jnp.zeros((8, x.shape[1]), F32)
    for i in range(XT):
        loads[i + 1].wait()
        sl = slice(i * xr, (i + 1) * xr)
        q[sl] = jnp.dot(x[sl], bdt[...], preferred_element_type=F32).astype(BF)
        sums = sums + jnp.dot(wrow[:, sl].astype(BF), x[sl], preferred_element_type=F32)
    sums_q = jnp.dot(wrow.astype(BF), q[...], preferred_element_type=F32)
    cart = x.shape[1]
    sz[zz, :, :cart] = sums[0:1]
    sz[zz, :, cart : cart + PANEL] = sums_q[0:1]
    sz[zz, :, cart + PANEL :] = jnp.broadcast_to(jnp.sum(wrow[0:1], axis=1, keepdims=True), (1, 128))
    sz_copies = [remote(sz.at[zz], sz.at[zz], z_s.at[o - 1], z_r.at[o - 1], z_peer(o)) for o in range(1, NZ)]
    for cp in sz_copies:
        cp.start()

    v_up.wait_recv()
    f_up = remote(ball.at[c_dn, hi], ball.at[c_dn, hi], val_s.at[3], val_r.at[3], x_up)
    f_up.start()
    s_dn = remote(ball.at[c_dn], ball.at[c_dn], val_s.at[4], val_r.at[4], sib)
    s_dn.start()
    v_dn.wait_recv()
    f_dn = remote(ball.at[c_up, lo], ball.at[c_up, lo], val_s.at[5], val_r.at[5], x_dn)
    f_dn.start()
    s_up = remote(ball.at[c_up], ball.at[c_up], val_s.at[6], val_r.at[6], sib)
    s_up.start()

    for cp in sz_copies:
        cp.wait_recv()
    part = sz[0]
    for j in range(1, NZ):
        part = part + sz[j]
    sy[yy] = part
    sy_copies = [remote(sy.at[yy], sy.at[yy], y_s.at[o - 1], y_r.at[o - 1], y_peer(o)) for o in range(1, NY)]
    for cp in sy_copies:
        cp.start()
    wcol = jnp.broadcast_to(wrow[0:1], (128, rows_total)).T
    for cp in sy_copies:
        cp.wait_recv()
    whole = sy[0]
    for j in range(1, NY):
        whole = whole + sy[j]
    count_ref[...] = whole[:, cart + PANEL :]
    inverse = 1.0 / whole[:, cart + PANEL : cart + PANEL + 1]
    mean = whole[:, cart : cart + PANEL] / whole[:, cart + PANEL : cart + PANEL + 1]
    mean_ref[...] = mean
    xm[...] = whole[:, :cart] * inverse
    wide = jnp.concatenate([wcol] * (PANEL // 128), axis=1)
    q[...] = (wide * (q[...].astype(F32) - mean)).astype(BF)

    GT = 384

    def g_tile(i, carry):
        start = pl.multiple_of(i * GT, 128)
        moved = (x[:, pl.ds(start, GT)].astype(F32) - xm[:, pl.ds(start, GT)]).astype(BF)
        tile = lax.dot_general(
            moved, q[...], (((0,), (0,)), ((), ())), preferred_element_type=F32
        ).astype(BF)
        for b in range(GT // BLOCK):
            g[i * (GT // BLOCK) + b] = tile[b * BLOCK : (b + 1) * BLOCK]
        return carry

    lax.fori_loop(0, x.shape[1] // GT, g_tile, 0)

    f_up.wait_recv()
    f_dn.wait_recv()
    s_op = remote(ball.at[c_op], ball.at[c_op], val_s.at[7], val_r.at[7], sib)
    s_op.start()
    for cp in col_copies:
        cp.wait_recv()
    own_cols.wait()
    to_smem = pltpu.make_async_copy(cbuf, csm, loc_sem.at[1])
    to_smem.start()
    own_vals.wait()
    to_smem.wait()
    for cp in (v_sib, s_dn, s_up, s_op):
        cp.wait_recv()

    def p_tile(i, carry):
        yr, zr = i // NZ, lax.rem(i, NZ)
        for h in range(2):
            panel, row = i // 4, lax.rem(i, 4) * 2 + h
            picked = jnp.concatenate(
                [g[csm[panel, row, k]] for k in range(8)], axis=0
            )
            out = jnp.dot(ball[panel, row], picked, preferred_element_type=F32).astype(BF)
            pa[yr, zr, h * BLOCK : (h + 1) * BLOCK] = out[:, : PANEL // 2]
            pb[zr, yr, h * BLOCK : (h + 1) * BLOCK] = out[:, PANEL // 2 :]
        return carry

    lax.fori_loop(0, NF, p_tile, 0)

    ring_ay = Ring(NY, yy, lambda t: (t * NZ + zz, c), pa, ay, ay_s, ay_r, NZ)
    ring_bz = Ring(NZ, zz, lambda t: (yy * NZ + t, c), pb, bz, bz_s, bz_r, NY)
    for d in range(2):
        ring_ay.start(d, 0)
        ring_bz.start(d, 0)
    for d in range(2):
        ring_bz.start(d, 1)
    for d in range(2):
        ring_ay.start(d, 1)
    for s in (2, 3):
        for d in range(2):
            ring_bz.start(d, s)
    ring_ay.finish()
    ra[...] = ring_ay.total().astype(BF)
    az_copies = [
        remote(ra.at[lax.rem(zz + o, NZ)], az.at[o - 1], az_s.at[o - 1], az_r.at[o - 1], z_peer(o)) for o in range(1, NZ)
    ]
    for cp in az_copies:
        cp.start()
    ring_bz.finish()
    rb[...] = ring_bz.total().astype(BF)
    by_copies = [
        remote(rb.at[lax.rem(yy + o, NY)], by.at[o - 1], by_s.at[o - 1], by_r.at[o - 1], y_peer(o)) for o in range(1, NY)
    ]
    for cp in by_copies:
        cp.start()
    scale = 1.0 / (whole[:, cart + PANEL : cart + PANEL + 1] - 1.0)
    total = ra[zz].astype(F32)
    for o in range(1, NZ):
        az_copies[o - 1].wait_recv()
        total = total + az[o - 1].astype(F32)
    cov_ref[:, : PANEL // 2] = total * scale
    total = rb[yy].astype(F32)
    for o in range(1, NY):
        by_copies[o - 1].wait_recv()
        total = total + by[o - 1].astype(F32)
    cov_ref[:, PANEL // 2 :] = total * scale

    for ring in (ring_ay, ring_bz):
        ring.drain()
    for cp in (v_up, v_dn, v_sib, f_up, f_dn, s_dn, s_up, s_op, *col_copies, *sz_copies, *sy_copies, *az_copies, *by_copies):
        cp.wait_send()


def on_device(frames, b_values, b_cols, frame_window):
    rows, cart = frames.shape
    vmem = pl.BlockSpec(memory_space=pltpu.VMEM)
    hbm = pl.BlockSpec(memory_space=pl.ANY)
    bdt = pl.pallas_call(
        densify,
        out_shape=jax.ShapeDtypeStruct((cart, PANEL), BF),
        in_specs=[pl.BlockSpec(memory_space=pltpu.SMEM), vmem],
        out_specs=vmem,
        name="densify",
    )(b_cols, b_values)
    cols = jnp.pad(b_cols, ((0, 0), (0, 120)))
    wrow = jnp.broadcast_to(frame_window.reshape(1, rows), (8, rows))
    dma = pltpu.SemaphoreType.DMA
    count, mean, cov = pl.pallas_call(
        main_kernel,
        out_shape=(
            jax.ShapeDtypeStruct((1, 128), F32),
            jax.ShapeDtypeStruct((1, PANEL), F32),
            jax.ShapeDtypeStruct((OWN, PANEL), F32),
        ),
        in_specs=[hbm, hbm, vmem, vmem, vmem],
        out_specs=(vmem, vmem, vmem),
        scratch_shapes=[
            pltpu.VMEM((rows, cart), BF),
            pltpu.VMEM((cart, PANEL), BF),
            pltpu.VMEM((rows, PANEL), BF),
            pltpu.VMEM((cart // BLOCK, BLOCK, PANEL), BF),
            pltpu.VMEM((NC, 8, BLOCK, PANEL), BF),
            pltpu.VMEM((NC, 8, 128), jnp.int32),
            pltpu.SMEM((NC, 8, 128), jnp.int32),
            pltpu.VMEM((NZ, 1, cart + PANEL + 128), F32),
            pltpu.VMEM((NY, 1, cart + PANEL + 128), F32),
            pltpu.VMEM((1, cart), F32),
            pltpu.VMEM((NY, NZ, OWN, PANEL // 2), BF),
            pltpu.VMEM((NZ, NY, OWN, PANEL // 2), BF),
            pltpu.VMEM((NZ, OWN, PANEL // 2), BF),
            pltpu.VMEM((NY, OWN, PANEL // 2), BF),
            pltpu.VMEM((2, NY // 2, NZ, OWN, PANEL // 2), BF),
            pltpu.VMEM((NZ - 1, OWN, PANEL // 2), BF),
            pltpu.VMEM((2, NZ // 2, NY, OWN, PANEL // 2), BF),
            pltpu.VMEM((NY - 1, OWN, PANEL // 2), BF),
            dma((5,)), dma((2,)), dma((8,)), dma((8,)), dma((7,)), dma((7,)),
            dma((NZ - 1,)), dma((NZ - 1,)), dma((NY - 1,)), dma((NY - 1,)),
            dma((2, NY // 2)), dma((2, NY // 2)), dma((NZ - 1,)), dma((NZ - 1,)),
            dma((2, NZ // 2)), dma((2, NZ // 2)), dma((NY - 1,)), dma((NY - 1,)),
        ],
        compiler_params=pltpu.CompilerParams(
            collective_id=0, has_side_effects=True, vmem_limit_bytes=60 * 1024 * 1024
        ),
        name="covariance",
    )(frames, bdt, b_values.reshape(8, BLOCK, PANEL), cols, wrow)
    return count[0, 0], mean.reshape(PANEL), cov


def solution(mesh):
    return jax.shard_map(
        on_device,
        mesh=mesh,
        in_specs=(P("frame", None), P("coord", None), P("coord", None), P("frame")),
        out_specs=(P(), P("coord"), P("frame", "coord")),
        check_vma=False,
    )
```

time: 415 us -> 99.4 us (0.24)
  waiting for transfers between devices: 275 us -> 0 us
  Pallas kernels: 0 us -> 90.1 us
  blocking collectives: 78.6 us -> 0 us
  matrix products: 17.2 us -> 0 us
  local copies, waits for them, and re-layouts: 22 us -> 5.51 us
  between operations: 14.7 us -> 2.39 us
  other arithmetic: 7.07 us -> 0 us
    reduce_scatter x1 -> x0, waiting for transfers between devices: 231 us -> none  [on_device(): lax.psum_scatter(lax.dot_general(centered_full, centered_mine, (((0,), (0...]
    pallas_call x0 -> x2, Pallas kernels: none -> 90.1 us  [the longest x1 86.6 us: on_device(): pl.pallas_call(main_kernel, out_shape=(jax.ShapeDtypeStruct((1, 128), F32...]
    psum x1 -> x0, blocking collectives: 78.6 us -> none  [on_device(): count, col_sums = lax.psum((local_count, local_sums), 'frame')]
    all_gather x1 -> x0, waiting for transfers between devices: 44.2 us -> none  [on_device(): centered_full = lax.all_gather(centered_mine, 'coord', axis=1, tiled=True)]
    dot_general x3 -> x0, matrix products: 17.2 us -> none  [the longest x1 11.4 us: on_device(): lax.dot_general(centered_full, centered_mine, (((0,), (0,)), ((), ())), p...]
    unnamed x5 -> x2, local copies, waits for them, and re-layouts: 12.4 us -> 2.92 us
    gather x1 -> x0, local copies, waits for them, and re-layouts: 9.02 us -> none  [project(): picked = jnp.take(blocks, col_blocks, axis=1)]
  transfers between devices with their start and end apart: 2 -> 0, of which waited for: 2 -> 0; matrix products, arithmetic and copies ran while one was open for 0% -> 0% of each run, Pallas kernels for 0% -> 0%
where the time goes in v1:
time: 99.4 us; the launch traced here: 98 us
  Pallas kernels  90.1 us (91%)
  local copies, waits for them, and re-layouts  5.51 us (6%)
  between operations  2.39 us (2%)
    pallas_call x1, Pallas kernels, on_device(): pl.pallas_call(main_kernel, out_shape=(jax.ShapeDtypeStruct((1, 128), F32...  86.6 us
    pallas_call x1, Pallas kernels, on_device(): pl.pallas_call(densify, out_shape=jax.ShapeDtypeStruct((cart, PANEL), BF)...  3.47 us
    unnamed x2, local copies, waits for them, and re-layouts  2.92 us

profile of v1, /device:TPU:6, one launch (start us, length us, event | category | flops | bytes accessed | tf_op | source)
XLA Modules:
  0.0 98.0 jit_solution(3345731571624968577)
XLA Ops:
  0.6 1.3 %pad.4.cols_ref = s32[8,128]{1,0:T(8,128)} pad(s32[8,8]{1,0:T(8,128)} %cols_ref.1, s32[]{:T(128)} %constant.0.clone.1), padding=0_0x0_120 | pad | bytes 4356 | tf_op jit(solution)/shard_map/jit(_pad)/pad | solution.py:291
  1.9 1.3 %broadcast_in_dim.2.wrow_ref = s32[8,1024]{1,0:T(8,128)} broadcast(s32[1024]{0:T(1024)} %param.7), dimensions={1} | broadcast | bytes 36864 | tf_op jit(solution)/shard_map/broadcast_in_dim | solution.py:292
  3.2 3.5 %densify.1.bdt_hbm = bf16[4224,512]{1,0:T(8,128)(2,1)} custom-call(s32[8,8]{1,0:T(8,128)} %cols_ref.1, bf16[512,512]{1,0:T(8,128)(2,1)} %vals_ref.1), custom_call_target="tpu_custom_call" | custom-call | tf_op jit(solution)/shard_map/densify/pallas_call | solution.py:284
  6.7 86.6 %covariance.1 = (f32[1,128]{1,0:T(1,128)}, f32[1,512]{1,0:T(1,128)}, f32[128,512]{1,0:T(8,128)}) custom-call(bf16[1024,4224]{1,0:T(8,128)(2,1)} %x_hbm.1, bf16[4224,512]{1,0:T(8,128)(2,1)} %densify.1.bdt_hbm, bf16[8,64,512]{2,1,0:T(8,128)(2,1)} %bitcast.4, s32[8,128]{1,0:T(8,128)} %pad.4.cols_ref, s32[8,1024]{1,0:T(8,128)} %broadcast_in_dim.2.wrow_ref), custom_call_target="tpu_custom_call" | custom-call | tf_op jit(solution)/shard_map/covariance/pallas_call | solution.py:294
  94.0 1.3 %copy.11 = f32[512]{0:T(512)} copy(f32[512]{0:T(512)} %bitcast.5) | data formatting | bytes 4096
  95.2 1.7 %copy.12 = f32[128,512]{1,0:T(8,128)} copy(f32[128,512]{1,0:T(8,128)} %get-tuple-element.14) | data formatting | bytes 524288

commit v2 on v1

--- a/solution.py
+++ b/solution.py
@@ -12,13 +12,17 @@
 NF, NC = NY * NZ, NX * 2
 PANEL = 512
 OWN = 128
+LANES = 128
+NA = 3
 MESH = pl.DeviceIdType.MESH
 BF = jnp.bfloat16
 F32 = jnp.float32
 
 
-def densify(cols_ref, vals_ref, out_ref):
+def densify(cols_ref, cols_vec_ref, vals_ref, out_ref, wide_cols_ref):
     out_ref[...] = jnp.zeros_like(out_ref)
+    wide_cols_ref[:, 0:8] = cols_vec_ref[...]
+    wide_cols_ref[:, 8:] = jnp.zeros((8, 120), jnp.int32)
     turned = vals_ref[...].T
     for r in range(8):
         lanes = slice(r * BLOCK, (r + 1) * BLOCK)
@@ -87,8 +91,8 @@
 def main_kernel(
     x_hbm, bdt_hbm, vals_ref, cols_ref, wrow_ref,
     count_ref, mean_ref, cov_ref,
-    x, bdt, q, g, ball, cbuf, csm, sz, sy, xm, pa, pb, ra, rb, ay, az, bz, by,
-    ld_sem, loc_sem, val_s, val_r, col_s, col_r, z_s, z_r, y_s, y_r,
+    x, bdt, q, g, ball, cbuf, csm, xz, xy, sz, sy, xm, pa, pb, ra, rb, ay, az, bz, by,
+    ld_sem, loc_sem, val_s, val_r, col_s, col_r, xz_s, xz_r, xy_s, xy_r, z_s, z_r, y_s, y_r,
     ay_s, ay_r, az_s, az_r, bz_s, bz_r, by_s, by_r,
 ):
     f, c = lax.axis_index("frame"), lax.axis_index("coord")
@@ -141,21 +145,41 @@
         cp.start()
 
     loads[0].wait()
-    wrow = wrow_ref[...].astype(F32)
+    wrow = jnp.broadcast_to(wrow_ref[...].astype(F32), (8, rows_total))
+    whalf = wrow.astype(BF)
     sums = jnp.zeros((8, x.shape[1]), F32)
+
+    def project(i):
+        sl = slice(i * xr, (i + 1) * xr)
+        q[sl] = jnp.dot(x[sl], bdt[...], preferred_element_type=F32).astype(BF)
+
     for i in range(XT):
         loads[i + 1].wait()
         sl = slice(i * xr, (i + 1) * xr)
-        q[sl] = jnp.dot(x[sl], bdt[...], preferred_element_type=F32).astype(BF)
-        sums = sums + jnp.dot(wrow[:, sl].astype(BF), x[sl], preferred_element_type=F32)
-    sums_q = jnp.dot(wrow.astype(BF), q[...], preferred_element_type=F32)
-    cart = x.shape[1]
-    sz[zz, :, :cart] = sums[0:1]
-    sz[zz, :, cart : cart + PANEL] = sums_q[0:1]
-    sz[zz, :, cart + PANEL :] = jnp.broadcast_to(jnp.sum(wrow[0:1], axis=1, keepdims=True), (1, 128))
-    sz_copies = [remote(sz.at[zz], sz.at[zz], z_s.at[o - 1], z_r.at[o - 1], z_peer(o)) for o in range(1, NZ)]
-    for cp in sz_copies:
-        cp.start()
+        sums = sums + jnp.dot(whalf[:, sl], x[sl], preferred_element_type=F32)
+        if i < XT - 1:
+            project(i)
+
+    def all_to_all(buf, mine, peer, n, send_sems, recv_sems):
+        copies = [remote(buf.at[mine], buf.at[mine], send_sems.at[o - 1], recv_sems.at[o - 1], peer(o)) for o in range(1, n)]
+        for cp in copies:
+            cp.start()
+        return copies
+
+    def gathered(buf, copies):
+        for cp in copies:
+            cp.wait_recv()
+        part = buf[0]
+        for j in range(1, buf.shape[0]):
+            part = part + buf[j]
+        return part
+
+    xz[zz] = sums[0:1]
+    xz_copies = all_to_all(xz, zz, z_peer, NZ, xz_s, xz_r)
+    project(XT - 1)
+    sz[zz, :, :PANEL] = jnp.dot(whalf, q[...], preferred_element_type=F32)[0:1]
+    sz[zz, :, PANEL:] = jnp.broadcast_to(jnp.sum(wrow[0:1], axis=1, keepdims=True), (1, 128))
+    sz_copies = all_to_all(sz, zz, z_peer, NZ, z_s, z_r)
 
     v_up.wait_recv()
     f_up = remote(ball.at[c_dn, hi], ball.at[c_dn, hi], val_s.at[3], val_r.at[3], x_up)
@@ -168,26 +192,18 @@
     s_up = remote(ball.at[c_up], ball.at[c_up], val_s.at[6], val_r.at[6], sib)
     s_up.start()
 
-    for cp in sz_copies:
-        cp.wait_recv()
-    part = sz[0]
-    for j in range(1, NZ):
-        part = part + sz[j]
-    sy[yy] = part
-    sy_copies = [remote(sy.at[yy], sy.at[yy], y_s.at[o - 1], y_r.at[o - 1], y_peer(o)) for o in range(1, NY)]
-    for cp in sy_copies:
-        cp.start()
+    xy[yy] = gathered(xz, xz_copies)
+    xy_copies = all_to_all(xy, yy, y_peer, NY, xy_s, xy_r)
+    sy[yy] = gathered(sz, sz_copies)
+    sy_copies = all_to_all(sy, yy, y_peer, NY, y_s, y_r)
     wcol = jnp.broadcast_to(wrow[0:1], (128, rows_total)).T
-    for cp in sy_copies:
-        cp.wait_recv()
-    whole = sy[0]
-    for j in range(1, NY):
-        whole = whole + sy[j]
-    count_ref[...] = whole[:, cart + PANEL :]
-    inverse = 1.0 / whole[:, cart + PANEL : cart + PANEL + 1]
-    mean = whole[:, cart : cart + PANEL] / whole[:, cart + PANEL : cart + PANEL + 1]
+    whole_x = gathered(xy, xy_copies)
+    whole = gathered(sy, sy_copies)
+    count_ref[...] = whole[:, PANEL:]
+    count = whole[:, PANEL : PANEL + 1]
+    mean = whole[:, :PANEL] / count
     mean_ref[...] = mean
-    xm[...] = whole[:, :cart] * inverse
+    xm[...] = whole_x * (1.0 / count)
     wide = jnp.concatenate([wcol] * (PANEL // 128), axis=1)
     q[...] = (wide * (q[...].astype(F32) - mean)).astype(BF)
 
@@ -219,61 +235,93 @@
     for cp in (v_sib, s_dn, s_up, s_op):
         cp.wait_recv()
 
-    def p_tile(i, carry):
-        yr, zr = i // NZ, lax.rem(i, NZ)
+    def p_tile(yr, zr):
+        panel = yr * 2 + zr // 4
         for h in range(2):
-            panel, row = i // 4, lax.rem(i, 4) * 2 + h
-            picked = jnp.concatenate(
-                [g[csm[panel, row, k]] for k in range(8)], axis=0
-            )
+            row = lax.rem(zr, 4) * 2 + h
+            picked = jnp.concatenate([g[csm[panel, row, k]] for k in range(8)], axis=0)
             out = jnp.dot(ball[panel, row], picked, preferred_element_type=F32).astype(BF)
-            pa[yr, zr, h * BLOCK : (h + 1) * BLOCK] = out[:, : PANEL // 2]
-            pb[zr, yr, h * BLOCK : (h + 1) * BLOCK] = out[:, PANEL // 2 :]
-        return carry
-
-    lax.fori_loop(0, NF, p_tile, 0)
-
-    ring_ay = Ring(NY, yy, lambda t: (t * NZ + zz, c), pa, ay, ay_s, ay_r, NZ)
-    ring_bz = Ring(NZ, zz, lambda t: (yy * NZ + t, c), pb, bz, bz_s, bz_r, NY)
-    for d in range(2):
-        ring_ay.start(d, 0)
-        ring_bz.start(d, 0)
-    for d in range(2):
-        ring_bz.start(d, 1)
-    for d in range(2):
-        ring_ay.start(d, 1)
-    for s in (2, 3):
+            sl = slice(h * BLOCK, (h + 1) * BLOCK)
+            for a in range(NA):
+                pa[a, yr, zr, sl] = out[:, a * LANES : (a + 1) * LANES]
+            pb[zr, yr, sl] = out[:, NA * LANES :]
+
+    def tiles(n, where):
+        def step(i, carry):
+            p_tile(*where(i))
+            return carry
+
+        lax.fori_loop(0, n, step, 0)
+
+    def y_at(o):
+        return lax.rem(yy + o, NY)
+
+    def z_at(o):
+        return lax.rem(zz + o, NZ)
+
+    ring_a = [
+        Ring(NY, yy, lambda t: (t * NZ + zz, c), pa.at[a], ay.at[a], ay_s.at[a], ay_r.at[a], NZ) for a in range(NA)
+    ]
+    ring_b = Ring(NZ, zz, lambda t: (yy * NZ + t, c), pb, bz, bz_s, bz_r, NY)
+
+    def both(ring, s):
         for d in range(2):
-            ring_bz.start(d, s)
-    ring_ay.finish()
-    ra[...] = ring_ay.total().astype(BF)
-    az_copies = [
-        remote(ra.at[lax.rem(zz + o, NZ)], az.at[o - 1], az_s.at[o - 1], az_r.at[o - 1], z_peer(o)) for o in range(1, NZ)
-    ]
-    for cp in az_copies:
-        cp.start()
-    ring_bz.finish()
-    rb[...] = ring_bz.total().astype(BF)
-    by_copies = [
-        remote(rb.at[lax.rem(yy + o, NY)], by.at[o - 1], by_s.at[o - 1], by_r.at[o - 1], y_peer(o)) for o in range(1, NY)
-    ]
+            ring.start(d, s)
+
+    tiles(NZ, lambda i: (y_at(2), i))
+    for a in range(NA):
+        both(ring_a[a], 0)
+    tiles(NY - 1, lambda i: (y_at(i + 3), z_at(4)))
+    both(ring_b, 0)
+    tiles(NZ - 1, lambda i: (y_at(1), z_at(i + 5)))
+    tiles(NZ - 1, lambda i: (y_at(3), z_at(i + 5)))
+    both(ring_a[0], 1)
+    tiles(NZ - 1, lambda i: (yy, z_at(i + 5)))
+    both(ring_b, 1)
+    both(ring_a[1], 1)
+    both(ring_b, 2)
+    both(ring_a[2], 1)
+    both(ring_b, 3)
+
+    az_copies, by_copies = [], []
+
+    def second(a):
+        ring_a[a].finish()
+        ra[a] = ring_a[a].total().astype(BF)
+        az_copies.append(
+            [remote(ra.at[a, z_at(o)], az.at[a, o - 1], az_s.at[a, o - 1], az_r.at[a, o - 1], z_peer(o)) for o in range(1, NZ)]
+        )
+        for cp in az_copies[a]:
+            cp.start()
+
+    second(0)
+    ring_b.finish()
+    rb[...] = ring_b.total().astype(BF)
+    for o in range(1, NY):
+        by_copies.append(remote(rb.at[y_at(o)], by.at[o - 1], by_s.at[o - 1], by_r.at[o - 1], y_peer(o)))
     for cp in by_copies:
         cp.start()
-    scale = 1.0 / (whole[:, cart + PANEL : cart + PANEL + 1] - 1.0)
-    total = ra[zz].astype(F32)
-    for o in range(1, NZ):
-        az_copies[o - 1].wait_recv()
-        total = total + az[o - 1].astype(F32)
-    cov_ref[:, : PANEL // 2] = total * scale
+    for a in range(1, NA):
+        second(a)
+    scale = 1.0 / (count - 1.0)
     total = rb[yy].astype(F32)
     for o in range(1, NY):
         by_copies[o - 1].wait_recv()
         total = total + by[o - 1].astype(F32)
-    cov_ref[:, PANEL // 2 :] = total * scale
-
-    for ring in (ring_ay, ring_bz):
+    cov_ref[:, NA * LANES :] = total * scale
+    for a in range(NA):
+        total = ra[a, zz].astype(F32)
+        for o in range(1, NZ):
+            az_copies[a][o - 1].wait_recv()
+            total = total + az[a, o - 1].astype(F32)
+        cov_ref[:, a * LANES : (a + 1) * LANES] = total * scale
+
+    for ring in (*ring_a, ring_b):
         ring.drain()
-    for cp in (v_up, v_dn, v_sib, f_up, f_dn, s_dn, s_up, s_op, *col_copies, *sz_copies, *sy_copies, *az_copies, *by_copies):
+    for copies in (*az_copies, by_copies, xz_copies, xy_copies, sz_copies, sy_copies, col_copies):
+        for cp in copies:
+            cp.wait_send()
+    for cp in (v_up, v_dn, v_sib, f_up, f_dn, s_dn, s_up, s_op):
         cp.wait_send()
 
 
@@ -281,15 +329,14 @@
     rows, cart = frames.shape
     vmem = pl.BlockSpec(memory_space=pltpu.VMEM)
     hbm = pl.BlockSpec(memory_space=pl.ANY)
-    bdt = pl.pallas_call(
+    bdt, cols = pl.pallas_call(
         densify,
-        out_shape=jax.ShapeDtypeStruct((cart, PANEL), BF),
-        in_specs=[pl.BlockSpec(memory_space=pltpu.SMEM), vmem],
-        out_specs=vmem,
+        out_shape=(jax.ShapeDtypeStruct((cart, PANEL), BF), jax.ShapeDtypeStruct((8, 128), jnp.int32)),
+        in_specs=[pl.BlockSpec(memory_space=pltpu.SMEM), vmem, vmem],
+        out_specs=(vmem, vmem),
         name="densify",
-    )(b_cols, b_values)
-    cols = jnp.pad(b_cols, ((0, 0), (0, 120)))
-    wrow = jnp.broadcast_to(frame_window.reshape(1, rows), (8, rows))
+    )(b_cols, b_cols, b_values)
+    wrow = frame_window.reshape(1, rows)
     dma = pltpu.SemaphoreType.DMA
     count, mean, cov = pl.pallas_call(
         main_kernel,
@@ -308,20 +355,23 @@
             pltpu.VMEM((NC, 8, BLOCK, PANEL), BF),
             pltpu.VMEM((NC, 8, 128), jnp.int32),
             pltpu.SMEM((NC, 8, 128), jnp.int32),
-            pltpu.VMEM((NZ, 1, cart + PANEL + 128), F32),
-            pltpu.VMEM((NY, 1, cart + PANEL + 128), F32),
+            pltpu.VMEM((NZ, 1, cart), F32),
+            pltpu.VMEM((NY, 1, cart), F32),
+            pltpu.VMEM((NZ, 1, PANEL + 128), F32),
+            pltpu.VMEM((NY, 1, PANEL + 128), F32),
             pltpu.VMEM((1, cart), F32),
-            pltpu.VMEM((NY, NZ, OWN, PANEL // 2), BF),
-            pltpu.VMEM((NZ, NY, OWN, PANEL // 2), BF),
-            pltpu.VMEM((NZ, OWN, PANEL // 2), BF),
-            pltpu.VMEM((NY, OWN, PANEL // 2), BF),
-            pltpu.VMEM((2, NY // 2, NZ, OWN, PANEL // 2), BF),
-            pltpu.VMEM((NZ - 1, OWN, PANEL // 2), BF),
-            pltpu.VMEM((2, NZ // 2, NY, OWN, PANEL // 2), BF),
-            pltpu.VMEM((NY - 1, OWN, PANEL // 2), BF),
+            pltpu.VMEM((NA, NY, NZ, OWN, LANES), BF),
+            pltpu.VMEM((NZ, NY, OWN, LANES), BF),
+            pltpu.VMEM((NA, NZ, OWN, LANES), BF),
+            pltpu.VMEM((NY, OWN, LANES), BF),
+            pltpu.VMEM((NA, 2, NY // 2, NZ, OWN, LANES), BF),
+            pltpu.VMEM((NA, NZ - 1, OWN, LANES), BF),
+            pltpu.VMEM((2, NZ // 2, NY, OWN, LANES), BF),
+            pltpu.VMEM((NY - 1, OWN, LANES), BF),
             dma((5,)), dma((2,)), dma((8,)), dma((8,)), dma((7,)), dma((7,)),
             dma((NZ - 1,)), dma((NZ - 1,)), dma((NY - 1,)), dma((NY - 1,)),
-            dma((2, NY // 2)), dma((2, NY // 2)), dma((NZ - 1,)), dma((NZ - 1,)),
+            dma((NZ - 1,)), dma((NZ - 1,)), dma((NY - 1,)), dma((NY - 1,)),
+            dma((NA, 2, NY // 2)), dma((NA, 2, NY // 2)), dma((NA, NZ - 1)), dma((NA, NZ - 1)),
             dma((2, NZ // 2)), dma((2, NZ // 2)), dma((NY - 1,)), dma((NY - 1,)),
         ],
         compiler_params=pltpu.CompilerParams(

time: 99.4 us -> 90.3 us (0.908)
  Pallas kernels: 90.1 us -> 84.4 us
  local copies, waits for them, and re-layouts: 5.51 us -> 2.92 us
    pallas_call x1, Pallas kernels: 86.6 us -> 80.9 us  [on_device(): pl.pallas_call(main_kernel, out_shape=(jax.ShapeDtypeStruct((1, 128), F32...]
    broadcast_in_dim x1 -> x0, local copies, waits for them, and re-layouts: 1.3 us -> none  [on_device(): wrow = jnp.broadcast_to(frame_window.reshape(1, rows), (8, rows))]
    pad x1 -> x0, local copies, waits for them, and re-layouts: 1.28 us -> none  [on_device(): cols = jnp.pad(b_cols, ((0, 0), (0, 120)))]
where the time goes in v2:
time: 90.3 us; the launch traced here: 89.7 us
  Pallas kernels  84.4 us (93%)
  local copies, waits for them, and re-layouts  2.92 us (3%)
  between operations  2.39 us (3%)
    pallas_call x1, Pallas kernels, on_device(): pl.pallas_call(main_kernel, out_shape=(jax.ShapeDtypeStruct((1, 128), F32...  80.9 us
    pallas_call x1, Pallas kernels, on_device(): pl.pallas_call(densify, out_shape=(jax.ShapeDtypeStruct((cart, PANEL), BF...  3.49 us
    unnamed x2, local copies, waits for them, and re-layouts  2.92 us

profile of v2, /device:TPU:6, one launch (start us, length us, event | category | flops | bytes accessed | tf_op | source)
XLA Modules:
  0.0 89.7 jit_solution(18424784813768085264)
XLA Ops:
  0.6 3.5 %densify.1 = (bf16[4224,512]{1,0:T(8,128)(2,1)}, s32[8,128]{1,0:T(8,128)}) custom-call(s32[8,8]{1,0:T(8,128)} %cols_vec_ref.1, s32[8,8]{1,0:T(8,128)} %cols_vec_ref.1, bf16[512,512]{1,0:T(8,128)(2,1)} %vals_ref.1), custom_call_target="tpu_custom_call" | custom-call | tf_op jit(solution)/shard_map/densify/pallas_call | solution.py:332
  4.1 80.9 %covariance.1 = (f32[1,128]{1,0:T(1,128)}, f32[1,512]{1,0:T(1,128)}, f32[128,512]{1,0:T(8,128)}) custom-call(bf16[1024,4224]{1,0:T(8,128)(2,1)} %x_hbm.1, bf16[4224,512]{1,0:T(8,128)(2,1)} %get-tuple-element.8.bdt_hbm, bf16[8,64,512]{2,1,0:T(8,128)(2,1)} %bitcast.5, s32[8,128]{1,0:T(8,128)} %get-tuple-element.9.cols_ref, s32[1,1024]{1,0:T(1,128)} %bitcast.6), custom_call_target="tpu_custom_call" | custom-call | tf_op jit(solution)/shard_map/covariance/pallas_call | solution.py:341
  85.7 1.3 %copy.11 = f32[512]{0:T(512)} copy(f32[512]{0:T(512)} %bitcast.7) | data formatting | bytes 4096
  86.9 1.7 %copy.12 = f32[128,512]{1,0:T(8,128)} copy(f32[128,512]{1,0:T(8,128)} %get-tuple-element.18) | data formatting | bytes 524288

commit v3 on v2

--- a/solution.py
+++ b/solution.py
@@ -181,6 +181,10 @@
     sz[zz, :, PANEL:] = jnp.broadcast_to(jnp.sum(wrow[0:1], axis=1, keepdims=True), (1, 128))
     sz_copies = all_to_all(sz, zz, z_peer, NZ, z_s, z_r)
 
+    xy[yy] = gathered(xz, xz_copies)
+    xy_copies = all_to_all(xy, yy, y_peer, NY, xy_s, xy_r)
+    sy[yy] = gathered(sz, sz_copies)
+    sy_copies = all_to_all(sy, yy, y_peer, NY, y_s, y_r)
     v_up.wait_recv()
     f_up = remote(ball.at[c_dn, hi], ball.at[c_dn, hi], val_s.at[3], val_r.at[3], x_up)
     f_up.start()
@@ -192,10 +196,6 @@
     s_up = remote(ball.at[c_up], ball.at[c_up], val_s.at[6], val_r.at[6], sib)
     s_up.start()
 
-    xy[yy] = gathered(xz, xz_copies)
-    xy_copies = all_to_all(xy, yy, y_peer, NY, xy_s, xy_r)
-    sy[yy] = gathered(sz, sz_copies)
-    sy_copies = all_to_all(sy, yy, y_peer, NY, y_s, y_r)
     wcol = jnp.broadcast_to(wrow[0:1], (128, rows_total)).T
     whole_x = gathered(xy, xy_copies)
     whole = gathered(sy, sy_copies)

time: 90.3 us -> 88.9 us (0.984)
  Pallas kernels: 84.4 us -> 83.4 us
    pallas_call x1, Pallas kernels: 80.9 us -> 79.9 us  [on_device(): pl.pallas_call(main_kernel, out_shape=(jax.ShapeDtypeStruct((1, 128), F32...]
where the time goes in v3:
time: 88.9 us; the launch traced here: 88.7 us
  Pallas kernels  83.4 us (94%)
  local copies, waits for them, and re-layouts  2.92 us (3%)
  between operations  2.39 us (3%)
    pallas_call x1, Pallas kernels, on_device(): pl.pallas_call(main_kernel, out_shape=(jax.ShapeDtypeStruct((1, 128), F32...  79.9 us
    pallas_call x1, Pallas kernels, on_device(): pl.pallas_call(densify, out_shape=(jax.ShapeDtypeStruct((cart, PANEL), BF...  3.49 us
    unnamed x2, local copies, waits for them, and re-layouts  2.92 us

profile of v3, /device:TPU:6, one launch (start us, length us, event | category | flops | bytes accessed | tf_op | source)
XLA Modules:
  0.0 88.7 jit_solution(17563255194776181710)
XLA Ops:
  0.6 3.5 %densify.1 = (bf16[4224,512]{1,0:T(8,128)(2,1)}, s32[8,128]{1,0:T(8,128)}) custom-call(s32[8,8]{1,0:T(8,128)} %cols_vec_ref.1, s32[8,8]{1,0:T(8,128)} %cols_vec_ref.1, bf16[512,512]{1,0:T(8,128)(2,1)} %vals_ref.1), custom_call_target="tpu_custom_call" | custom-call | tf_op jit(solution)/shard_map/densify/pallas_call | solution.py:332
  4.1 79.9 %covariance.1 = (f32[1,128]{1,0:T(1,128)}, f32[1,512]{1,0:T(1,128)}, f32[128,512]{1,0:T(8,128)}) custom-call(bf16[1024,4224]{1,0:T(8,128)(2,1)} %x_hbm.1, bf16[4224,512]{1,0:T(8,128)(2,1)} %get-tuple-element.8.bdt_hbm, bf16[8,64,512]{2,1,0:T(8,128)(2,1)} %bitcast.5, s32[8,128]{1,0:T(8,128)} %get-tuple-element.9.cols_ref, s32[1,1024]{1,0:T(1,128)} %bitcast.6), custom_call_target="tpu_custom_call" | custom-call | tf_op jit(solution)/shard_map/covariance/pallas_call | solution.py:341
  84.7 1.3 %copy.11 = f32[512]{0:T(512)} copy(f32[512]{0:T(512)} %bitcast.7) | data formatting | bytes 4096
  85.9 1.7 %copy.12 = f32[128,512]{1,0:T(8,128)} copy(f32[128,512]{1,0:T(8,128)} %get-tuple-element.18) | data formatting | bytes 524288

commit v4 on v3

--- a/solution.py
+++ b/solution.py
@@ -14,6 +14,7 @@
 OWN = 128
 LANES = 128
 NA = 3
+UNIT = 72
 MESH = pl.DeviceIdType.MESH
 BF = jnp.bfloat16
 F32 = jnp.float32
@@ -91,9 +92,9 @@
 def main_kernel(
     x_hbm, bdt_hbm, vals_ref, cols_ref, wrow_ref,
     count_ref, mean_ref, cov_ref,
-    x, bdt, q, g, ball, cbuf, csm, xz, xy, sz, sy, xm, pa, pb, ra, rb, ay, az, bz, by,
+    x, bdt, q, g, ball, cbuf, csm, xz, xy, sz, sy, xm, pa, pb, ra, rb, ay, az, bz, by, fr, land,
     ld_sem, loc_sem, val_s, val_r, col_s, col_r, xz_s, xz_r, xy_s, xy_r, z_s, z_r, y_s, y_r,
-    ay_s, ay_r, az_s, az_r, bz_s, bz_r, by_s, by_r,
+    ay_s, ay_r, az_s, az_r, bz_s, bz_r, by_s, by_r, fin_s, fin_r,
 ):
     f, c = lax.axis_index("frame"), lax.axis_index("coord")
     yy, zz = f // NZ, lax.rem(f, NZ)
@@ -235,23 +236,42 @@
     for cp in (v_sib, s_dn, s_up, s_op):
         cp.wait_recv()
 
-    def p_tile(yr, zr):
-        panel = yr * 2 + zr // 4
-        for h in range(2):
-            row = lax.rem(zr, 4) * 2 + h
-            picked = jnp.concatenate([g[csm[panel, row, k]] for k in range(8)], axis=0)
-            out = jnp.dot(ball[panel, row], picked, preferred_element_type=F32).astype(BF)
-            sl = slice(h * BLOCK, (h + 1) * BLOCK)
-            for a in range(NA):
-                pa[a, yr, zr, sl] = out[:, a * LANES : (a + 1) * LANES]
-            pb[zr, yr, sl] = out[:, NA * LANES :]
-
-    def tiles(n, where):
-        def step(i, carry):
-            p_tile(*where(i))
+    def p_rows(panel, row, lanes):
+        picked = jnp.concatenate([g[csm[panel, row, k], :, lanes] for k in range(8)], axis=0)
+        return jnp.dot(ball[panel, row], picked, preferred_element_type=F32)
+
+    def keep(j, t, z, rows, value):
+        if j < NA:
+            pa[j, t, z, rows] = value.astype(BF)
+        else:
+            pb[z, t, rows] = value.astype(BF)
+
+    def near_blocks(pair):
+        def step(z, carry):
+            panel = lax.rem(c + z // 2, NC)
+            for p in range(2):
+                for h in range(2):
+                    row = (lax.rem(z, 2) * 2 + p) * 2 + h
+                    out = p_rows(panel, row, slice(pair * 256, pair * 256 + 256))
+                    for tt in range(2):
+                        for jj in range(2):
+                            part = out[tt * 32 : tt * 32 + 32, jj * LANES : (jj + 1) * LANES]
+                            keep(pair * 2 + jj, 2 * h + tt, z, slice(p * 32, p * 32 + 32), part)
             return carry
 
-        lax.fori_loop(0, n, step, 0)
+        lax.fori_loop(0, NZ, step, 0)
+
+    def far_block(j, e):
+        return lax.rem(j + 4 - e - c // 4, 4)
+
+    def far_blocks(j):
+        for e in range(2):
+            for h in range(2):
+                out = p_rows(c_op, far_block(j, e) * 2 + h, slice(j * LANES, (j + 1) * LANES))
+                for tt in range(2):
+                    for zq in range(4):
+                        part = out[tt * 32 + zq * 8 : tt * 32 + zq * 8 + 8]
+                        keep(j, 2 * h + tt, 4 * e + zq, slice(64, 72), part)
 
     def y_at(o):
         return lax.rem(yy + o, NY)
@@ -268,20 +288,21 @@
         for d in range(2):
             ring.start(d, s)
 
-    tiles(NZ, lambda i: (y_at(2), i))
-    for a in range(NA):
-        both(ring_a[a], 0)
-    tiles(NY - 1, lambda i: (y_at(i + 3), z_at(4)))
+    near_blocks(0)
+    for j in range(2):
+        far_blocks(j)
+        both(ring_a[j], 0)
+    near_blocks(1)
+    far_blocks(3)
     both(ring_b, 0)
-    tiles(NZ - 1, lambda i: (y_at(1), z_at(i + 5)))
-    tiles(NZ - 1, lambda i: (y_at(3), z_at(i + 5)))
+    far_blocks(2)
+    both(ring_a[2], 0)
+    both(ring_b, 1)
     both(ring_a[0], 1)
-    tiles(NZ - 1, lambda i: (yy, z_at(i + 5)))
-    both(ring_b, 1)
+    both(ring_b, 2)
     both(ring_a[1], 1)
-    both(ring_b, 2)
+    both(ring_b, 3)
     both(ring_a[2], 1)
-    both(ring_b, 3)
 
     az_copies, by_copies = [], []
 
@@ -304,17 +325,67 @@
     for a in range(1, NA):
         second(a)
     scale = 1.0 / (count - 1.0)
+    sent = []
+
+    def place(j, n, src, dst_rows, delta, block, mirrored):
+        row_panel = lax.rem(c + delta, NC)
+        target = row_panel * 4 + block
+        dst = land.at[j, dst_rows]
+        here = make_local(src, dst, fin_r.at[j])
+        there = remote(src, dst, fin_s.at[j, n], fin_r.at[j], (target, c))
+        same = target == f
+
+        @pl.when(same)
+        def _():
+            here.start()
+
+        @pl.when(jnp.logical_not(same))
+        def _():
+            there.start()
+
+        sent.append((jnp.logical_not(same), there))
+        turned = remote(src, land.at[block, dst_rows], fin_s.at[j, n + 3], fin_r.at[block], (c * 4 + j, row_panel))
+
+        @pl.when(mirrored)
+        def _():
+            turned.start()
+
+        sent.append((mirrored, turned))
+
+    def make_local(src, dst, sem):
+        return pltpu.make_async_copy(src, dst, sem)
+
+    def deliver(j, total):
+        fr[j] = (total * scale).reshape(UNIT // 8, 8, LANES)
+        for p in range(2):
+            place(j, p, fr.at[j, pl.ds(4 * p, 4)], pl.ds(4 * yy, 4), zz // 2, lax.rem(zz, 2) * 2 + p, zz >= 2)
+        e = zz // 4
+        place(j, 2, fr.at[j, pl.ds(8, 1)], pl.ds(4 * yy + lax.rem(zz, 4), 1), 4, far_block(j, e), zz >= 0)
+
     total = rb[yy].astype(F32)
     for o in range(1, NY):
         by_copies[o - 1].wait_recv()
         total = total + by[o - 1].astype(F32)
-    cov_ref[:, NA * LANES :] = total * scale
+    deliver(NA, total)
     for a in range(NA):
         total = ra[a, zz].astype(F32)
         for o in range(1, NZ):
             az_copies[a][o - 1].wait_recv()
             total = total + az[a, o - 1].astype(F32)
-        cov_ref[:, a * LANES : (a + 1) * LANES] = total * scale
+        deliver(a, total)
+
+    delta = lax.rem(f // 4 - c + NC, NC)
+    for j in range(NA + 1):
+        remote(land.at[j], land.at[j], fin_s.at[j, 0], fin_r.at[j], sib).wait_recv()
+        block = land[j].reshape(OWN, LANES)
+        off = lax.rem(j - lax.rem(f, 4) + 4, 4) - c // 4
+        straight = jnp.where(delta == 4, jnp.logical_and(off >= 0, off <= 1), delta < 4)
+        cov_ref[:, j * LANES : (j + 1) * LANES] = jnp.where(straight, block, block.T)
+    for going, cp in sent:
+
+        @pl.when(going)
+        def _(cp=cp):
+            cp.wait_send()
 
     for ring in (*ring_a, ring_b):
         ring.drain()
@@ -360,19 +431,22 @@
             pltpu.VMEM((NZ, 1, PANEL + 128), F32),
             pltpu.VMEM((NY, 1, PANEL + 128), F32),
             pltpu.VMEM((1, cart), F32),
-            pltpu.VMEM((NA, NY, NZ, OWN, LANES), BF),
-            pltpu.VMEM((NZ, NY, OWN, LANES), BF),
-            pltpu.VMEM((NA, NZ, OWN, LANES), BF),
-            pltpu.VMEM((NY, OWN, LANES), BF),
-            pltpu.VMEM((NA, 2, NY // 2, NZ, OWN, LANES), BF),
-            pltpu.VMEM((NA, NZ - 1, OWN, LANES), BF),
-            pltpu.VMEM((2, NZ // 2, NY, OWN, LANES), BF),
-            pltpu.VMEM((NY - 1, OWN, LANES), BF),
+            pltpu.VMEM((NA, NY, NZ, UNIT, LANES), BF),
+            pltpu.VMEM((NZ, NY, UNIT, LANES), BF),
+            pltpu.VMEM((NA, NZ, UNIT, LANES), BF),
+            pltpu.VMEM((NY, UNIT, LANES), BF),
+            pltpu.VMEM((NA, 2, NY // 2, NZ, UNIT, LANES), BF),
+            pltpu.VMEM((NA, NZ - 1, UNIT, LANES), BF),
+            pltpu.VMEM((2, NZ // 2, NY, UNIT, LANES), BF),
+            pltpu.VMEM((NY - 1, UNIT, LANES), BF),
+            pltpu.VMEM((NA + 1, UNIT // 8, 8, LANES), F32),
+            pltpu.VMEM((NA + 1, OWN // 8, 8, LANES), F32),
             dma((5,)), dma((2,)), dma((8,)), dma((8,)), dma((7,)), dma((7,)),
             dma((NZ - 1,)), dma((NZ - 1,)), dma((NY - 1,)), dma((NY - 1,)),
             dma((NZ - 1,)), dma((NZ - 1,)), dma((NY - 1,)), dma((NY - 1,)),
             dma((NA, 2, NY // 2)), dma((NA, 2, NY // 2)), dma((NA, NZ - 1)), dma((NA, NZ - 1)),
             dma((2, NZ // 2)), dma((2, NZ // 2)), dma((NY - 1,)), dma((NY - 1,)),
+            dma((NA + 1, 6)), dma((NA + 1,)),
         ],
         compiler_params=pltpu.CompilerParams(
             collective_id=0, has_side_effects=True, vmem_limit_bytes=60 * 1024 * 1024

time: 88.9 us -> 84.3 us (0.948)
  the two profiles are of different devices: /device:TPU:6 before, /device:TPU:80 now
where the time goes in v4:
time: 84.3 us; the launch traced here: 84.1 us
  Pallas kernels  78.8 us (93%)
  local copies, waits for them, and re-layouts  2.92 us (3%)
  between operations  2.39 us (3%)
    pallas_call x1, Pallas kernels, on_device(): pl.pallas_call(main_kernel, out_shape=(jax.ShapeDtypeStruct((1, 128), F32...  75.3 us
    pallas_call x1, Pallas kernels, on_device(): pl.pallas_call(densify, out_shape=(jax.ShapeDtypeStruct((cart, PANEL), BF...  3.49 us
    unnamed x2, local copies, waits for them, and re-layouts  2.92 us

profile of v4, /device:TPU:80, one launch (start us, length us, event | category | flops | bytes accessed | tf_op | source)
XLA Modules:
  0.0 84.1 jit_solution(5322282516714657336)
XLA Ops:
  0.6 3.5 %densify.1 = (bf16[4224,512]{1,0:T(8,128)(2,1)}, s32[8,128]{1,0:T(8,128)}) custom-call(s32[8,8]{1,0:T(8,128)} %cols_vec_ref.1, s32[8,8]{1,0:T(8,128)} %cols_vec_ref.1, bf16[512,512]{1,0:T(8,128)(2,1)} %vals_ref.1), custom_call_target="tpu_custom_call" | custom-call | tf_op jit(solution)/shard_map/densify/pallas_call | solution.py:403
  4.1 75.3 %covariance.1 = (f32[1,128]{1,0:T(1,128)}, f32[1,512]{1,0:T(1,128)}, f32[128,512]{1,0:T(8,128)}) custom-call(bf16[1024,4224]{1,0:T(8,128)(2,1)} %x_hbm.1, bf16[4224,512]{1,0:T(8,128)(2,1)} %get-tuple-element.8.bdt_hbm, bf16[8,64,512]{2,1,0:T(8,128)(2,1)} %bitcast.5, s32[8,128]{1,0:T(8,128)} %get-tuple-element.9.cols_ref, s32[1,1024]{1,0:T(1,128)} %bitcast.6), custom_call_target="tpu_custom_call" | custom-call | tf_op jit(solution)/shard_map/covariance/pallas_call | solution.py:412
  80.0 1.3 %copy.11 = f32[512]{0:T(512)} copy(f32[512]{0:T(512)} %bitcast.7) | data formatting | bytes 4096
  81.3 1.7 %copy.12 = f32[128,512]{1,0:T(8,128)} copy(f32[128,512]{1,0:T(8,128)} %get-tuple-element.18) | data formatting | bytes 524288

commit v5 on v4

--- a/solution.py
+++ b/solution.py
@@ -15,21 +15,10 @@
 LANES = 128
 NA = 3
 UNIT = 72
+ROW = 640
 MESH = pl.DeviceIdType.MESH
 BF = jnp.bfloat16
 F32 = jnp.float32
-
-
-def densify(cols_ref, cols_vec_ref, vals_ref, out_ref, wide_cols_ref):
-    out_ref[...] = jnp.zeros_like(out_ref)
-    wide_cols_ref[:, 0:8] = cols_vec_ref[...]
-    wide_cols_ref[:, 8:] = jnp.zeros((8, 120), jnp.int32)
-    turned = vals_ref[...].T
-    for r in range(8):
-        lanes = slice(r * BLOCK, (r + 1) * BLOCK)
-        for k in range(8):
-            row = pl.multiple_of(cols_ref[r, k] * BLOCK, BLOCK)
-            out_ref[pl.ds(row, BLOCK), lanes] = turned[k * BLOCK : (k + 1) * BLOCK, lanes]
 
 
 def remote(src, dst, send_sem, recv_sem, device):
@@ -90,9 +79,9 @@
 
 
 def main_kernel(
-    x_hbm, bdt_hbm, vals_ref, cols_ref, wrow_ref,
+    x_hbm, vals_ref, cols_ref, wrow_ref,
     count_ref, mean_ref, cov_ref,
-    x, bdt, q, g, ball, cbuf, csm, xz, xy, sz, sy, xm, pa, pb, ra, rb, ay, az, bz, by, fr, land,
+    x, vt, found, where_sm, bdt, q, g, ball, cbuf, csm, rows8, xz, xy, sz, sy, xm, pa, pb, ra, rb, ay, az, bz, by, fr, land,
     ld_sem, loc_sem, val_s, val_r, col_s, col_r, xz_s, xz_r, xy_s, xy_r, z_s, z_r, y_s, y_r,
     ay_s, ay_r, az_s, az_r, bz_s, bz_r, by_s, by_r, fin_s, fin_r,
 ):
@@ -102,10 +91,10 @@
     rows_total = x.shape[0]
     XT = 4
     xr = rows_total // XT
-    loads = [pltpu.make_async_copy(bdt_hbm, bdt, ld_sem.at[0])]
+    loads = []
     for i in range(XT):
         sl = pl.ds(i * xr, xr)
-        loads.append(pltpu.make_async_copy(x_hbm.at[sl], x.at[sl], ld_sem.at[i + 1]))
+        loads.append(pltpu.make_async_copy(x_hbm.at[sl], x.at[sl], ld_sem.at[i]))
     for cp in loads:
         cp.start()
 
@@ -131,31 +120,49 @@
     c_up, c_dn, c_op = x_up[1], x_dn[1], lax.rem(c + 4, NC)
     lo, hi = pl.ds(0, 4), pl.ds(4, 4)
     own_vals = pltpu.make_async_copy(vals_ref, ball.at[c], loc_sem.at[0])
-    own_cols = pltpu.make_async_copy(cols_ref, cbuf.at[c], loc_sem.at[1])
     own_vals.start()
-    own_cols.start()
+    cbuf[c, :, 0:8] = cols_ref[...]
+    cbuf[c, :, 8:] = jnp.zeros((8, 120), jnp.int32)
     v_up = remote(vals_ref, ball.at[c], val_s.at[0], val_r.at[0], x_up)
     v_dn = remote(vals_ref, ball.at[c], val_s.at[1], val_r.at[1], x_dn)
     v_sib = remote(vals_ref, ball.at[c], val_s.at[2], val_r.at[2], sib)
     for cp in (v_up, v_dn, v_sib):
         cp.start()
     col_copies = [
-        remote(cols_ref, cbuf.at[c], col_s.at[o - 1], col_r.at[o - 1], coord_peer(o)) for o in range(1, NC)
+        remote(cbuf.at[c], cbuf.at[c], col_s.at[o - 1], col_r.at[o - 1], coord_peer(o)) for o in range(1, NC)
     ]
     for cp in col_copies:
         cp.start()
 
-    loads[0].wait()
+    lane = lax.broadcasted_iota(jnp.int32, (8, 128), 1)
+    holder = jnp.full((8, 128), 8, jnp.int32)
+    for k in range(8):
+        holder = jnp.where(cols_ref[:, k : k + 1] == lane, k, holder)
+    found[...] = holder
+    to_where = pltpu.make_async_copy(found, where_sm, loc_sem.at[2])
+    to_where.start()
+    vt[0:8] = vals_ref[...].reshape(PANEL, PANEL).T.reshape(8, BLOCK, PANEL)
+    vt[8] = jnp.zeros((BLOCK, PANEL), BF)
+    to_where.wait()
+
+    def spread(b, carry):
+        for r in range(8):
+            lanes = slice(r * BLOCK, (r + 1) * BLOCK)
+            bdt[b, :, lanes] = vt[where_sm[r, b], :, lanes]
+        return carry
+
+    lax.fori_loop(0, bdt.shape[0], spread, 0)
     wrow = jnp.broadcast_to(wrow_ref[...].astype(F32), (8, rows_total))
     whalf = wrow.astype(BF)
     sums = jnp.zeros((8, x.shape[1]), F32)
 
     def project(i):
         sl = slice(i * xr, (i + 1) * xr)
-        q[sl] = jnp.dot(x[sl], bdt[...], preferred_element_type=F32).astype(BF)
-
+        q[sl] = jnp.dot(x[sl], bdt[...].reshape(x.shape[1], PANEL), preferred_element_type=F32).astype(BF)
+
+    cart = x.shape[1]
     for i in range(XT):
-        loads[i + 1].wait()
+        loads[i].wait()
         sl = slice(i * xr, (i + 1) * xr)
         sums = sums + jnp.dot(whalf[:, sl], x[sl], preferred_element_type=F32)
         if i < XT - 1:
@@ -170,19 +177,22 @@
     def gathered(buf, copies):
         for cp in copies:
             cp.wait_recv()
-        part = buf[0]
+        part = buf[0].astype(F32)
         for j in range(1, buf.shape[0]):
-            part = part + buf[j]
+            part = part + buf[j].astype(F32)
         return part
 
-    xz[zz] = sums[0:1]
+    wide_sums = jnp.concatenate([sums[0:1], jnp.zeros((1, 8 * ROW - cart), F32)], axis=1)
+    for i in range(8):
+        rows8[i : i + 1] = wide_sums[:, i * ROW : (i + 1) * ROW]
+    xz[zz] = rows8[...].astype(BF)
     xz_copies = all_to_all(xz, zz, z_peer, NZ, xz_s, xz_r)
     project(XT - 1)
     sz[zz, :, :PANEL] = jnp.dot(whalf, q[...], preferred_element_type=F32)[0:1]
     sz[zz, :, PANEL:] = jnp.broadcast_to(jnp.sum(wrow[0:1], axis=1, keepdims=True), (1, 128))
     sz_copies = all_to_all(sz, zz, z_peer, NZ, z_s, z_r)
 
-    xy[yy] = gathered(xz, xz_copies)
+    xy[yy] = gathered(xz, xz_copies).astype(BF)
     xy_copies = all_to_all(xy, yy, y_peer, NY, xy_s, xy_r)
     sy[yy] = gathered(sz, sz_copies)
     sy_copies = all_to_all(sy, yy, y_peer, NY, y_s, y_r)
@@ -204,7 +214,11 @@
     count = whole[:, PANEL : PANEL + 1]
     mean = whole[:, :PANEL] / count
     mean_ref[...] = mean
-    xm[...] = whole_x * (1.0 / count)
+    whole_x = whole_x * (1.0 / count)
+    for i in range(8):
+        width = min(ROW, cart - i * ROW)
+        if width > 0:
+            xm[:, i * ROW : i * ROW + width] = whole_x[i : i + 1, :width]
     wide = jnp.concatenate([wcol] * (PANEL // 128), axis=1)
     q[...] = (wide * (q[...].astype(F32) - mean)).astype(BF)
 
@@ -228,7 +242,6 @@
     s_op.start()
     for cp in col_copies:
         cp.wait_recv()
-    own_cols.wait()
     to_smem = pltpu.make_async_copy(cbuf, csm, loc_sem.at[1])
     to_smem.start()
     own_vals.wait()
@@ -400,13 +413,6 @@
     rows, cart = frames.shape
     vmem = pl.BlockSpec(memory_space=pltpu.VMEM)
     hbm = pl.BlockSpec(memory_space=pl.ANY)
-    bdt, cols = pl.pallas_call(
-        densify,
-        out_shape=(jax.ShapeDtypeStruct((cart, PANEL), BF), jax.ShapeDtypeStruct((8, 128), jnp.int32)),
-        in_specs=[pl.BlockSpec(memory_space=pltpu.SMEM), vmem, vmem],
-        out_specs=(vmem, vmem),
-        name="densify",
-    )(b_cols, b_cols, b_values)
     wrow = frame_window.reshape(1, rows)
     dma = pltpu.SemaphoreType.DMA
     count, mean, cov = pl.pallas_call(
@@ -416,18 +422,22 @@
             jax.ShapeDtypeStruct((1, PANEL), F32),
             jax.ShapeDtypeStruct((OWN, PANEL), F32),
         ),
-        in_specs=[hbm, hbm, vmem, vmem, vmem],
+        in_specs=[hbm, vmem, vmem, vmem],
         out_specs=(vmem, vmem, vmem),
         scratch_shapes=[
             pltpu.VMEM((rows, cart), BF),
-            pltpu.VMEM((cart, PANEL), BF),
+            pltpu.VMEM((9, BLOCK, PANEL), BF),
+            pltpu.VMEM((8, 128), jnp.int32),
+            pltpu.SMEM((8, 128), jnp.int32),
+            pltpu.VMEM((cart // BLOCK, BLOCK, PANEL), BF),
             pltpu.VMEM((rows, PANEL), BF),
             pltpu.VMEM((cart // BLOCK, BLOCK, PANEL), BF),
             pltpu.VMEM((NC, 8, BLOCK, PANEL), BF),
             pltpu.VMEM((NC, 8, 128), jnp.int32),
             pltpu.SMEM((NC, 8, 128), jnp.int32),
-            pltpu.VMEM((NZ, 1, cart), F32),
-            pltpu.VMEM((NY, 1, cart), F32),
+            pltpu.VMEM((8, ROW), F32),
+            pltpu.VMEM((NZ, 8, ROW), BF),
+            pltpu.VMEM((NY, 8, ROW), BF),
             pltpu.VMEM((NZ, 1, PANEL + 128), F32),
             pltpu.VMEM((NY, 1, PANEL + 128), F32),
             pltpu.VMEM((1, cart), F32),
@@ -441,7 +451,7 @@
             pltpu.VMEM((NY - 1, UNIT, LANES), BF),
             pltpu.VMEM((NA + 1, UNIT // 8, 8, LANES), F32),
             pltpu.VMEM((NA + 1, OWN // 8, 8, LANES), F32),
-            dma((5,)), dma((2,)), dma((8,)), dma((8,)), dma((7,)), dma((7,)),
+            dma((4,)), dma((3,)), dma((8,)), dma((8,)), dma((7,)), dma((7,)),
             dma((NZ - 1,)), dma((NZ - 1,)), dma((NY - 1,)), dma((NY - 1,)),
             dma((NZ - 1,)), dma((NZ - 1,)), dma((NY - 1,)), dma((NY - 1,)),
             dma((NA, 2, NY // 2)), dma((NA, 2, NY // 2)), dma((NA, NZ - 1)), dma((NA, NZ - 1)),
@@ -452,7 +462,7 @@
             collective_id=0, has_side_effects=True, vmem_limit_bytes=60 * 1024 * 1024
         ),
         name="covariance",
-    )(frames, bdt, b_values.reshape(8, BLOCK, PANEL), cols, wrow)
+    )(frames, b_values.reshape(8, BLOCK, PANEL), b_cols, wrow)
     return count[0, 0], mean.reshape(PANEL), cov
 
 

time: 84.3 us -> 82.5 us (0.979)
  the two profiles are of different devices: /device:TPU:80 before, /device:TPU:6 now
where the time goes in v5:
time: 82.5 us; the launch traced here: 81.2 us
  Pallas kernels  76 us (92%)
  local copies, waits for them, and re-layouts  2.92 us (4%)
  between operations  2.31 us (3%)
    pallas_call x1, Pallas kernels, on_device(): pl.pallas_call(main_kernel, out_shape=(jax.ShapeDtypeStruct((1, 128), F32...  76 us
    unnamed x2, local copies, waits for them, and re-layouts  2.92 us

profile of v5, /device:TPU:6, one launch (start us, length us, event | category | flops | bytes accessed | tf_op | source)
XLA Modules:
  0.0 81.2 jit_solution(17699677818427617100)
XLA Ops:
  0.6 76.0 %covariance.1 = (f32[1,128]{1,0:T(1,128)}, f32[1,512]{1,0:T(1,128)}, f32[128,512]{1,0:T(8,128)}) custom-call(bf16[1024,4224]{1,0:T(8,128)(2,1)} %x_hbm.1, bf16[8,64,512]{2,1,0:T(8,128)(2,1)} %bitcast.5, s32[8,8]{1,0:T(8,128)} %cols_ref.1, s32[1,1024]{1,0:T(1,128)} %bitcast.6), custom_call_target="tpu_custom_call" | custom-call | tf_op jit(solution)/shard_map/covariance/pallas_call | solution.py:418
  77.2 1.2 %copy.11 = f32[512]{0:T(512)} copy(f32[512]{0:T(512)} %bitcast.7) | data formatting | bytes 4096
  78.4 1.7 %copy.12 = f32[128,512]{1,0:T(8,128)} copy(f32[128,512]{1,0:T(8,128)} %get-tuple-element.14) | data formatting | bytes 524288

commit v6 on v5

--- a/solution.py
+++ b/solution.py
@@ -118,15 +118,16 @@
     pl.semaphore_wait(barrier, len(peers))
 
     c_up, c_dn, c_op = x_up[1], x_dn[1], lax.rem(c + 4, NC)
-    lo, hi = pl.ds(0, 4), pl.ds(4, 4)
+    lo, hi = pl.ds(0, 3), pl.ds(3, 5)
     own_vals = pltpu.make_async_copy(vals_ref, ball.at[c], loc_sem.at[0])
     own_vals.start()
     cbuf[c, :, 0:8] = cols_ref[...]
     cbuf[c, :, 8:] = jnp.zeros((8, 120), jnp.int32)
-    v_up = remote(vals_ref, ball.at[c], val_s.at[0], val_r.at[0], x_up)
-    v_dn = remote(vals_ref, ball.at[c], val_s.at[1], val_r.at[1], x_dn)
+    v_up = remote(vals_ref.at[hi], ball.at[c, hi], val_s.at[0], val_r.at[0], x_up)
+    v_dn = remote(vals_ref.at[lo], ball.at[c, lo], val_s.at[1], val_r.at[1], x_dn)
+    v_dn_rest = remote(vals_ref.at[hi], ball.at[c, hi], val_s.at[4], val_r.at[4], x_dn)
     v_sib = remote(vals_ref, ball.at[c], val_s.at[2], val_r.at[2], sib)
-    for cp in (v_up, v_dn, v_sib):
+    for cp in (v_up, v_dn, v_dn_rest, v_sib):
         cp.start()
     col_copies = [
         remote(cbuf.at[c], cbuf.at[c], col_s.at[o - 1], col_r.at[o - 1], coord_peer(o)) for o in range(1, NC)
@@ -192,22 +193,21 @@
     sz[zz, :, PANEL:] = jnp.broadcast_to(jnp.sum(wrow[0:1], axis=1, keepdims=True), (1, 128))
     sz_copies = all_to_all(sz, zz, z_peer, NZ, z_s, z_r)
 
+    v_up.wait_recv()
+    f_up = remote(ball.at[c_dn, hi], ball.at[c_dn, hi], val_s.at[3], val_r.at[3], x_up)
+    f_up.start()
+    v_dn.wait_recv()
+    f_dn = remote(ball.at[c_up, lo], ball.at[c_up, lo], val_s.at[5], val_r.at[5], x_dn)
+    f_dn.start()
+
     xy[yy] = gathered(xz, xz_copies).astype(BF)
     xy_copies = all_to_all(xy, yy, y_peer, NY, xy_s, xy_r)
     sy[yy] = gathered(sz, sz_copies)
     sy_copies = all_to_all(sy, yy, y_peer, NY, y_s, y_r)
-    v_up.wait_recv()
-    f_up = remote(ball.at[c_dn, hi], ball.at[c_dn, hi], val_s.at[3], val_r.at[3], x_up)
-    f_up.start()
-    s_dn = remote(ball.at[c_dn], ball.at[c_dn], val_s.at[4], val_r.at[4], sib)
-    s_dn.start()
-    v_dn.wait_recv()
-    f_dn = remote(ball.at[c_up, lo], ball.at[c_up, lo], val_s.at[5], val_r.at[5], x_dn)
-    f_dn.start()
+    wcol = jnp.broadcast_to(wrow[0:1], (128, rows_total)).T
+    v_dn_rest.wait_recv()
     s_up = remote(ball.at[c_up], ball.at[c_up], val_s.at[6], val_r.at[6], sib)
     s_up.start()
-
-    wcol = jnp.broadcast_to(wrow[0:1], (128, rows_total)).T
     whole_x = gathered(xy, xy_copies)
     whole = gathered(sy, sy_copies)
     count_ref[...] = whole[:, PANEL:]
@@ -234,20 +234,30 @@
             g[i * (GT // BLOCK) + b] = tile[b * BLOCK : (b + 1) * BLOCK]
         return carry
 
-    lax.fori_loop(0, x.shape[1] // GT, g_tile, 0)
+    g_tiles = x.shape[1] // GT
+    lax.fori_loop(0, g_tiles - 3, g_tile, 0)
 
     f_up.wait_recv()
     f_dn.wait_recv()
     s_op = remote(ball.at[c_op], ball.at[c_op], val_s.at[7], val_r.at[7], sib)
-    s_op.start()
+
+    @pl.when(kk == 0)
+    def _():
+        s_op.start()
+
+    lax.fori_loop(g_tiles - 3, g_tiles, g_tile, 0)
     for cp in col_copies:
         cp.wait_recv()
     to_smem = pltpu.make_async_copy(cbuf, csm, loc_sem.at[1])
     to_smem.start()
     own_vals.wait()
     to_smem.wait()
-    for cp in (v_sib, s_dn, s_up, s_op):
+    for cp in (v_sib, s_up):
         cp.wait_recv()
+
+    @pl.when(kk == 1)
+    def _():
+        remote(ball.at[c_op - 1], ball.at[c_op - 1], val_s.at[7], val_r.at[7], sib).wait_recv()
 
     def p_rows(panel, row, lanes):
         picked = jnp.concatenate([g[csm[panel, row, k], :, lanes] for k in range(8)], axis=0)
@@ -405,8 +415,12 @@
     for copies in (*az_copies, by_copies, xz_copies, xy_copies, sz_copies, sy_copies, col_copies):
         for cp in copies:
             cp.wait_send()
-    for cp in (v_up, v_dn, v_sib, f_up, f_dn, s_dn, s_up, s_op):
+    for cp in (v_up, v_dn, v_dn_rest, v_sib, f_up, f_dn, s_up):
         cp.wait_send()
+
+    @pl.when(kk == 0)
+    def _():
+        s_op.wait_send()
 
 
 def on_device(frames, b_values, b_cols, frame_window):

time: 82.5 us -> 83.1 us (level)
  no operation moved by 1% of the time
where the time goes in v6:
time: 83.1 us; the launch traced here: 82 us
  Pallas kernels  76.7 us (92%)
  local copies, waits for them, and re-layouts  2.92 us (4%)
  between operations  2.31 us (3%)
    pallas_call x1, Pallas kernels, on_device(): pl.pallas_call(main_kernel, out_shape=(jax.ShapeDtypeStruct((1, 128), F32...  76.7 us
    unnamed x2, local copies, waits for them, and re-layouts  2.92 us

profile of v6, /device:TPU:6, one launch (start us, length us, event | category | flops | bytes accessed | tf_op | source)
XLA Modules:
  0.0 82.0 jit_solution(13412588434456557781)
XLA Ops:
  0.6 76.7 %covariance.1 = (f32[1,128]{1,0:T(1,128)}, f32[1,512]{1,0:T(1,128)}, f32[128,512]{1,0:T(8,128)}) custom-call(bf16[1024,4224]{1,0:T(8,128)(2,1)} %x_hbm.1, bf16[8,64,512]{2,1,0:T(8,128)(2,1)} %bitcast.5, s32[8,8]{1,0:T(8,128)} %cols_ref.1, s32[1,1024]{1,0:T(1,128)} %bitcast.6), custom_call_target="tpu_custom_call" | custom-call | tf_op jit(solution)/shard_map/covariance/pallas_call | solution.py:432
  77.9 1.2 %copy.11 = f32[512]{0:T(512)} copy(f32[512]{0:T(512)} %bitcast.7) | data formatting | bytes 4096
  79.2 1.7 %copy.12 = f32[128,512]{1,0:T(8,128)} copy(f32[128,512]{1,0:T(8,128)} %get-tuple-element.14) | data formatting | bytes 524288

commit v7 on v6

--- a/solution.py
+++ b/solution.py
@@ -80,7 +80,7 @@
 
 def main_kernel(
     x_hbm, vals_ref, cols_ref, wrow_ref,
-    count_ref, mean_ref, cov_ref,
+    sums_ref, cov_ref,
     x, vt, found, where_sm, bdt, q, g, ball, cbuf, csm, rows8, xz, xy, sz, sy, xm, pa, pb, ra, rb, ay, az, bz, by, fr, land,
     ld_sem, loc_sem, val_s, val_r, col_s, col_r, xz_s, xz_r, xy_s, xy_r, z_s, z_r, y_s, y_r,
     ay_s, ay_r, az_s, az_r, bz_s, bz_r, by_s, by_r, fin_s, fin_r,
@@ -115,6 +115,25 @@
     peers = [coord_peer(o) for o in range(1, NC)] + [z_peer(o) for o in range(1, NZ)] + [y_peer(o) for o in range(1, NY)]
     for p in peers:
         pl.semaphore_signal(barrier, inc=1, device_id=p, device_id_type=MESH)
+
+    lane = lax.broadcasted_iota(jnp.int32, (8, 128), 1)
+    holder = jnp.full((8, 128), 8, jnp.int32)
+    for k in range(8):
+        holder = jnp.where(cols_ref[:, k : k + 1] == lane, k, holder)
+    found[...] = holder
+    to_where = pltpu.make_async_copy(found, where_sm, loc_sem.at[2])
+    to_where.start()
+    vt[0:8] = vals_ref[...].reshape(PANEL, PANEL).T.reshape(8, BLOCK, PANEL)
+    vt[8] = jnp.zeros((BLOCK, PANEL), BF)
+    to_where.wait()
+
+    def spread(b, carry):
+        for r in range(8):
+            lanes = slice(r * BLOCK, (r + 1) * BLOCK)
+            bdt[b, :, lanes] = vt[where_sm[r, b], :, lanes]
+        return carry
+
+    lax.fori_loop(0, bdt.shape[0], spread, 0)
     pl.semaphore_wait(barrier, len(peers))
 
     c_up, c_dn, c_op = x_up[1], x_dn[1], lax.rem(c + 4, NC)
@@ -135,24 +154,6 @@
     for cp in col_copies:
         cp.start()
 
-    lane = lax.broadcasted_iota(jnp.int32, (8, 128), 1)
-    holder = jnp.full((8, 128), 8, jnp.int32)
-    for k in range(8):
-        holder = jnp.where(cols_ref[:, k : k + 1] == lane, k, holder)
-    found[...] = holder
-    to_where = pltpu.make_async_copy(found, where_sm, loc_sem.at[2])
-    to_where.start()
-    vt[0:8] = vals_ref[...].reshape(PANEL, PANEL).T.reshape(8, BLOCK, PANEL)
-    vt[8] = jnp.zeros((BLOCK, PANEL), BF)
-    to_where.wait()
-
-    def spread(b, carry):
-        for r in range(8):
-            lanes = slice(r * BLOCK, (r + 1) * BLOCK)
-            bdt[b, :, lanes] = vt[where_sm[r, b], :, lanes]
-        return carry
-
-    lax.fori_loop(0, bdt.shape[0], spread, 0)
     wrow = jnp.broadcast_to(wrow_ref[...].astype(F32), (8, rows_total))
     whalf = wrow.astype(BF)
     sums = jnp.zeros((8, x.shape[1]), F32)
@@ -210,10 +211,9 @@
     s_up.start()
     whole_x = gathered(xy, xy_copies)
     whole = gathered(sy, sy_copies)
-    count_ref[...] = whole[:, PANEL:]
+    sums_ref[...] = whole
     count = whole[:, PANEL : PANEL + 1]
     mean = whole[:, :PANEL] / count
-    mean_ref[...] = mean
     whole_x = whole_x * (1.0 / count)
     for i in range(8):
         width = min(ROW, cart - i * ROW)
@@ -347,7 +347,6 @@
         cp.start()
     for a in range(1, NA):
         second(a)
-    scale = 1.0 / (count - 1.0)
     sent = []
 
     def place(j, n, src, dst_rows, delta, block, mirrored):
@@ -379,7 +378,7 @@
         return pltpu.make_async_copy(src, dst, sem)
 
     def deliver(j, total):
-        fr[j] = (total * scale).reshape(UNIT // 8, 8, LANES)
+        fr[j] = total.reshape(UNIT // 8, 8, LANES)
         for p in range(2):
             place(j, p, fr.at[j, pl.ds(4 * p, 4)], pl.ds(4 * yy, 4), zz // 2, lax.rem(zz, 2) * 2 + p, zz >= 2)
         e = zz // 4
@@ -423,21 +422,27 @@
         s_op.wait_send()
 
 
+def finish(sums_ref, raw_ref, count_ref, mean_ref, cov_ref):
+    count = sums_ref[:, PANEL : PANEL + 1]
+    count_ref[...] = sums_ref[:, PANEL:]
+    mean_ref[...] = sums_ref[:, :PANEL] / count
+    cov_ref[...] = raw_ref[...] * (1.0 / (count - 1.0))
+
+
 def on_device(frames, b_values, b_cols, frame_window):
     rows, cart = frames.shape
     vmem = pl.BlockSpec(memory_space=pltpu.VMEM)
     hbm = pl.BlockSpec(memory_space=pl.ANY)
     wrow = frame_window.reshape(1, rows)
     dma = pltpu.SemaphoreType.DMA
-    count, mean, cov = pl.pallas_call(
+    sums, raw = pl.pallas_call(
         main_kernel,
         out_shape=(
-            jax.ShapeDtypeStruct((1, 128), F32),
-            jax.ShapeDtypeStruct((1, PANEL), F32),
+            jax.ShapeDtypeStruct((1, PANEL + 128), F32),
             jax.ShapeDtypeStruct((OWN, PANEL), F32),
         ),
         in_specs=[hbm, vmem, vmem, vmem],
-        out_specs=(vmem, vmem, vmem),
+        out_specs=(vmem, vmem),
         scratch_shapes=[
             pltpu.VMEM((rows, cart), BF),
             pltpu.VMEM((9, BLOCK, PANEL), BF),
@@ -477,6 +482,17 @@
         ),
         name="covariance",
     )(frames, b_values.reshape(8, BLOCK, PANEL), b_cols, wrow)
+    count, mean, cov = pl.pallas_call(
+        finish,
+        out_shape=(
+            jax.ShapeDtypeStruct((1, 128), F32),
+            jax.ShapeDtypeStruct((1, PANEL), F32),
+            jax.ShapeDtypeStruct((OWN, PANEL), F32),
+        ),
+        in_specs=[vmem, vmem],
+        out_specs=(vmem, vmem, vmem),
+        name="finish",
+    )(sums, raw)
     return count[0, 0], mean.reshape(PANEL), cov
 
 

time: 83.1 us -> 77.3 us (0.930)
  local copies, waits for them, and re-layouts: 2.92 us -> 0 us
  between operations: 2.31 us -> 0.64 us
    unnamed x2 -> x0, local copies, waits for them, and re-layouts: 2.92 us -> none
    pallas_call x1 -> x2, Pallas kernels: 76.7 us -> 75.9 us  [the longest x1 74.1 us: on_device(): pl.pallas_call(main_kernel, out_shape=(jax.ShapeDtypeStruct((1, PANEL + 1...]
where the time goes in v7:
time: 77.3 us; the launch traced here: 76.5 us
  Pallas kernels  75.9 us (98%)
    pallas_call x1, Pallas kernels, on_device(): pl.pallas_call(main_kernel, out_shape=(jax.ShapeDtypeStruct((1, PANEL + 1...  74.1 us
    pallas_call x1, Pallas kernels, on_device(): pl.pallas_call(finish, out_shape=(jax.ShapeDtypeStruct((1, 128), F32), ja...  1.75 us

profile of v7, /device:TPU:6, one launch (start us, length us, event | category | flops | bytes accessed | tf_op | source)
XLA Modules:
  0.0 76.5 jit_solution(17163500716969147342)
XLA Ops:
  0.6 74.1 %covariance.1 = (f32[1,640]{1,0:T(1,128)}, f32[128,512]{1,0:T(8,128)}) custom-call(bf16[1024,4224]{1,0:T(8,128)(2,1)} %x_hbm.1, bf16[8,64,512]{2,1,0:T(8,128)(2,1)} %bitcast.5, s32[8,8]{1,0:T(8,128)} %cols_ref.1, s32[1,1024]{1,0:T(1,128)} %bitcast.6), custom_call_target="tpu_custom_call" | custom-call | tf_op jit(solution)/shard_map/covariance/pallas_call | solution.py:438
  74.8 1.8 %finish.1 = (f32[1,128]{1,0:T(1,128)}, f32[1,512]{1,0:T(1,128)}, f32[128,512]{1,0:T(8,128)}) custom-call(f32[1,640]{1,0:T(1,128)} %get-tuple-element.8.sums_ref, f32[128,512]{1,0:T(8,128)} %get-tuple-element.9.raw_ref), custom_call_target="tpu_custom_call" | custom-call | tf_op jit(solution)/shard_map/finish/pallas_call | solution.py:485
